TPU v7x, 32 devices: a whole 2x2x4 slice. The times are simulated.
32 devices in a mesh: member: 2 (over y), wave: 4 (over z), level: 2 (over x), fld: 2 (over core).
Axes of the slice: x: 2, y: 2, z: 4, core: 2. Of those that a mesh axis runs over, the one named last changes fastest.
Arguments:
- grid_state: bfloat16 [256, 2, 256, 1536], P(('member', 'level'), 'fld', 'wave'), parts along dimension 0, may hold values from -6 to 6
- legendre: bfloat16 [512, 2, 256, 256], P(('wave', 'level'), 'fld'), may hold values from -0.375 to 0.375
- wave_order: int32 [512], replicated, may hold values from 0 to 511, each once
- lat_order: int32 [256], replicated, may hold values from 0 to 255, each once
- eig_rates: float32 [128], replicated, may hold values from 0.1 to 4
- modes_in: bfloat16 [128, 128], replicated, may hold values from -0.5 to 0.5
- modes_out: bfloat16 [128, 128], replicated, may hold values from -0.5 to 0.5
Outputs:
- new_state: bfloat16 [256, 2, 256, 1536], P(('member', 'level'), 'fld', 'wave'), parts along dimension 0
There are 2 independent parts, one for each index of `member`. A program takes and returns all parts, laid end to end along the dimension named above; an argument that names none is the same for every part. Nothing has to cross between parts.
Inputs may be any that keep to these rules, and one draw needn't show every extreme that they name: Slot s holds zonal wavenumber wave_order[s]; every wavenumber 0 to 511 is held by exactly one slot. Latitude row r lies at Gaussian latitude index lat_order[r] counted from the equator, the same in both hemispheres; every index appears once.
All inputs are finite; a program needn't handle non-finite values.
Results may differ from a plain program's by a relative error of at most 0.0098.
Values may be sent and summed in bfloat16 or wider, within the bound.
No kernel may reach another device: no remote copies, remote signals or barrier semaphores. Data moves between devices by JAX's collectives and lax.ppermute only.
A program may use at most 128 MiB of HBM per device.

v0:
```python
import math
import jax
import jax.numpy as jnp
from jax import lax
from jax.sharding import PartitionSpec as P

tau_scale = 2.0


def partner(value, axis, stride):
    mask = 2**stride
    pairs = [(source, source ^ mask) for source in range(lax.axis_size(axis))]
    return lax.ppermute(value, axis, pairs)


def fourier_table(wave_order, lon_count):
    longitude = jnp.arange(lon_count, dtype=jnp.int32)
    phase_index = longitude[:, None] * wave_order[None, :] % lon_count
    angles = phase_index.astype(jnp.float32) * (2.0 * math.pi / lon_count)
    weight_scale = math.sqrt(2.0 / lon_count)
    return jnp.concatenate(
        [jnp.cos(angles) * weight_scale, -jnp.sin(angles) * weight_scale], axis=1
    ).astype(jnp.bfloat16)


def degrees(wave_ids, parity, half_count):
    return wave_ids[:, None] + 2 * jnp.arange(half_count, dtype=jnp.int32)[None, :] + parity


def triangle_mask(wave_ids, parity, half_count, wave_count):
    return (degrees(wave_ids, parity, half_count) <= wave_count - 1).astype(jnp.float32)


def damping(wave_ids, parity, half_count, wave_count, eig_rates):
    degree_f = degrees(wave_ids, parity, half_count).astype(jnp.float32)
    damp_ratio = tau_scale * degree_f * (degree_f + 1.0) / float(wave_count * (wave_count - 1))
    return 1.0 / (1.0 + damp_ratio[:, :, None] * eig_rates[None, None, :])


def forward_legendre(mirrored, table_part, in_triangle):
    spectral = jnp.einsum(
        "lhrcs,shrj->sjcl", mirrored, table_part, preferred_element_type=jnp.float32
    )
    return (spectral * in_triangle[:, :, None, None]).astype(jnp.bfloat16)


def inverse_legendre(solved, table_part):
    return jnp.einsum(
        "sjcl,shrj->lhrcs", solved, table_part, preferred_element_type=jnp.float32
    ).astype(jnp.bfloat16)


def implicit_solve(columns, factor, modes_in, modes_out):
    modal = jnp.einsum("sjcl,kl->sjck", columns, modes_in, preferred_element_type=jnp.float32)
    modal = (modal * factor[:, :, None, :]).astype(jnp.bfloat16)
    return jnp.einsum("sjck,lk->sjcl", modal, modes_out, preferred_element_type=jnp.float32).astype(
        jnp.bfloat16
    )


def shards(grid_state, legendre, wave_order, lat_order, eig_rates, modes_in, modes_out):
    lon_count = grid_state.shape[3]
    rows_here = grid_state.shape[2]
    wave_count = wave_order.shape[0]
    half_rows = lat_order.shape[0]
    half_count = legendre.shape[3]
    wave_size = lax.axis_size("wave")
    level_size = lax.axis_size("level")
    parity = lax.axis_index("fld")
    wave_place = lax.axis_index("wave")
    level_place = lax.axis_index("level")
    wave_table = fourier_table(wave_order, lon_count)
    lat_rows = lax.dynamic_slice_in_dim(lat_order, wave_place * rows_here, rows_here)
    sine = jnp.sin((lat_rows.astype(jnp.float32) + 0.5) * (math.pi / (2.0 * half_rows)))
    hemi_sign = 1.0 - 2.0 * parity.astype(jnp.float32)
    coupling = (0.5 * hemi_sign * sine)[None, None, :, None]
    wide_count = wave_count // wave_size
    narrow_count = wide_count // level_size
    wide_start = wave_place * wide_count
    narrow_start = wide_start + level_place * narrow_count
    wide_waves = lax.dynamic_slice_in_dim(wave_order, wide_start, wide_count)
    narrow_waves = lax.dynamic_slice_in_dim(wave_order, narrow_start, narrow_count)
    factor = damping(narrow_waves, parity, half_count, wave_count, eig_rates)
    wide_table = lax.all_gather(legendre, "level", axis=0, tiled=True)
    wide_mask = triangle_mask(wide_waves, parity, half_count, wave_count)
    initial = grid_state.astype(jnp.float32)
    current = grid_state
    forcing = (initial + coupling * jnp.tanh(current.astype(jnp.float32))).astype(jnp.bfloat16)
    fourier_rows = jnp.einsum(
        "lhrg,gk->lhrk", forcing, wave_table, preferred_element_type=jnp.float32
    )
    fourier_rows = fourier_rows.astype(jnp.bfloat16).reshape(
        fourier_rows.shape[:3] + (2, wave_count)
    )
    mirror_part = partner(fourier_rows, "fld", 0)
    mirrored = (
        mirror_part.astype(jnp.float32) + hemi_sign * fourier_rows.astype(jnp.float32)
    ).astype(jnp.bfloat16)
    gathered = lax.all_to_all(mirrored, "wave", split_axis=4, concat_axis=2, tiled=True)
    spectral = forward_legendre(gathered, wide_table, wide_mask)
    columns = lax.all_to_all(spectral, "level", split_axis=0, concat_axis=3, tiled=True)
    solved = implicit_solve(columns, factor, modes_in, modes_out)
    level_rows = lax.all_to_all(solved, "level", split_axis=3, concat_axis=0, tiled=True)
    grid_coeffs = inverse_legendre(level_rows, wide_table)
    grid_coeffs = lax.all_to_all(grid_coeffs, "wave", split_axis=2, concat_axis=4, tiled=True)
    mirror_back = partner(grid_coeffs, "fld", 0)
    hemi_grid = (
        0.5 * (mirror_back.astype(jnp.float32) + hemi_sign * grid_coeffs.astype(jnp.float32))
    ).astype(jnp.bfloat16)
    flat_coeffs = hemi_grid.reshape(hemi_grid.shape[:3] + (2 * wave_count,))
    current = jnp.einsum(
        "lhrk,gk->lhrg", flat_coeffs, wave_table, preferred_element_type=jnp.float32
    ).astype(jnp.bfloat16)
    return current


def solution(mesh):
    placed = (
        P(("member", "level"), "fld", "wave", None),
        P(("wave", "level"), "fld", None, None),
        P(),
        P(),
        P(),
        P(),
        P(),
    )
    return jax.shard_map(
        shards,
        mesh=mesh,
        in_specs=placed,
        out_specs=P(("member", "level"), "fld", "wave", None),
        check_vma=False,
    )
```

profile of v0, /device:TPU:0, one launch (start us, length us, event | category | flops | bytes accessed | tf_op | source)
XLA Modules:
  0.0 995.7 jit_solution(6568454296517900749)
XLA Ops:
  6.5 0.0 copy-start
  6.5 0.0 all-gather.2.cloned.1.call-start
  6.5 14.1 %multiply_convert_fusion.4 = (bf16[1536,512]{1,0:T(8,128)(2,1)S(1)}, bf16[1536,512]{1,0:T(8,128)(2,1)S(1)}) fusion(s32[512]{0:T(512)} %param.9), kind=kLoop, calls=%fused_computation.28 | loop fusion | flops 11010048 | bytes 3147776 | tf_op jit(solution)/shard_map/convert
  20.6 0.0 copy-start.2
  20.7 0.0 copy-start.4
  20.7 0.8 sine_multiply_fusion
  21.5 18.9 %fusion.13 = bf16[64,64,1024]{2,1,0:T(8,128)(2,1)} fusion(bf16[64,1,64,1536]{3,2,1,0:T(8,128)(2,1)} %param.7, f32[64]{0:T(128)S(1)} %sine_multiply_fusion, bf16[1536,512]{1,0:T(8,128)(2,1)S(1)} %get-tuple-element.6, bf16[1536,512]{1,0:T(8,128)(2,1)S(1)} %get-tuple-element.5), kind=kOutput, calls=%fused_computation.21 | convolution fusion | flops 12920553472 | bytes 24117504 | tf_op jit(solution)/shard_map/lhrg,gk->lhrk/dot_general | solution.py:89
  40.4 0.0 copy-done.2
  40.4 0.0 copy-done.4
  40.4 14.5 %reshape.138 = bf16[64,1,64,2,512]{4,3,2,0,1:T(2,128)(2,1)} reshape(bf16[64,64,1024]{2,1,0:T(8,128)(2,1)} %fusion.13) | data formatting | bytes 16777216 | tf_op jit(solution)/shard_map/reshape | solution.py:92
  54.9 9.0 copy.61
  64.0 0.5 collective-permute-start
  64.5 0.0 all-gather.2.cloned.1.call-update
  64.5 13.1 %collective-permute-done = bf16[64,1,64,2,512]{4,2,3,0,1:T(8,128)(2,1)} collective-permute-done((bf16[64,1,64,2,512]{4,2,3,0,1:T(8,128)(2,1)}, bf16[64,1,64,2,512]{4,2,3,0,1:T(8,128)(2,1)}, u32[]{:S(2)}, u32[]{:S(2)}) %collective-permute-start) | collective-permute-done | bytes 8388640 | tf_op jit(solution)/shard_map/ppermute | solution.py:13
  77.6 12.1 %add_convert_fusion = bf16[64,1,64,2,512]{4,2,3,0,1:T(8,128)(2,1)} fusion(bf16[64,1,64,2,512]{4,2,3,0,1:T(8,128)(2,1)} %collective-permute-done, f32[]{:T(128)S(6)} %sub.3, bf16[64,1,64,2,512]{4,3,2,0,1:T(2,128)(2,1)} %reshape.138), kind=kLoop, calls=%fused_computation.11 | loop fusion | flops 20971520 | bytes 25165828 | tf_op jit(solution)/shard_map/convert_element_type | solution.py:98
  89.7 34.4 %copy.63 = bf16[64,1,64,2,512]{2,3,0,1,4:T(2,128)(2,1)} copy(bf16[64,1,64,2,512]{4,2,3,0,1:T(8,128)(2,1)} %add_convert_fusion) | data formatting | bytes 16777216 | tf_op jit(solution)/shard_map/convert_element_type | solution.py:98
  124.1 16.8 %reshape.146 = bf16[4,2,524288]{2,1,0:T(2,128)(2,1)} reshape(bf16[512,1,64,2,64]{4,3,2,1,0:T(2,128)(2,1)} %bitcast.76) | data formatting | bytes 16777216
  140.9 0.0 copy-start.7
  140.9 6.2 all-to-all-start
  147.2 0.0 copy-done.7
  147.2 0.1 dynamic_slice.10
  147.2 0.1 fusion.26
  147.3 184.2 %all-to-all-done = bf16[4,2,524288]{2,1,0:T(2,128)(2,1)} async-done(((bf16[4,2,524288]{2,1,0:T(2,128)(2,1)}), bf16[4,2,524288]{2,1,0:T(2,128)(2,1)}, u32[]{:S(2)}, u32[]{:S(2)}) %all-to-all-start) | async-done | bytes 8388640 | tf_op jit(solution)/shard_map/all_to_all | solution.py:99
  331.6 16.0 %reshape.147 = bf16[512,1,64,2,64]{4,3,2,1,0:T(2,128)(2,1)} reshape(bf16[4,2,524288]{2,1,0:T(2,128)(2,1)} %all-to-all-done) | data formatting | bytes 16777216
  347.5 41.2 %copy.81 = bf16[64,1,64,2,4,128]{5,4,2,3,0,1:T(4,128)(2,1)} copy(bf16[64,1,64,2,4,128]{2,3,0,5,4,1:T(2,128)(2,1)} %bitcast.77) | data formatting | bytes 16777216 | tf_op jit(solution)/shard_map/all_to_all | solution.py:99
  388.7 9.3 copy.65
  398.0 12.1 %copy.66 = bf16[64,256,2,128]{1,0,2,3:T(8,128)(2,1)} copy(bf16[64,256,2,128]{3,1,2,0:T(8,128)(2,1)} %bitcast.81) | data formatting | bytes 16777216 | tf_op jit(solution)/shard_map/reshape.6
  410.1 0.0 all-gather.2.cloned.1.call-done
  410.1 15.1 %fusion.18 = bf16[128,256,2,64]{1,3,2,0:T(8,128)(2,1)} fusion(f32[128,256]{1,0:T(8,128)S(1)} %fusion.26, bf16[64,256,2,128]{1,0,2,3:T(8,128)(2,1)} %copy.66, bf16[128,1,256,256]{3,2,1,0:T(8,128)(2,1)} %all-gather.2.cloned.1.call-done), kind=kOutput, calls=%fused_computation.22 | convolution fusion | flops 2155872256 | bytes 33685504 | tf_op jit(solution)/shard_map/lhrcs,shrj->sjcl/dot_general | solution.py:41
  425.2 0.0 copy-start.8
  425.2 7.1 all-to-all-start.1
  432.4 0.1 dynamic_slice.11
  432.4 0.1 multiply_multiply_fusion
  432.5 0.0 copy-done.8
  432.5 15.2 %add_divide_fusion = f32[64,256,128]{2,1,0:T(8,128)} fusion(f32[128]{0:T(128)S(1)} %copy-done.8, f32[64,256]{1,0:T(8,128)S(1)} %multiply_multiply_fusion), kind=kLoop, calls=%fused_computation.19 | loop fusion | flops 6291456 | bytes 8454656 | tf_op jit(solution)/shard_map/div | solution.py:37
  447.7 77.0 %all-to-all-done.1 = bf16[128,256,2,64]{1,3,2,0:T(8,128)(2,1)} async-done(((bf16[128,256,2,64]{1,3,2,0:T(8,128)(2,1)}), bf16[128,256,2,64]{1,3,2,0:T(8,128)(2,1)}, u32[]{:S(2)}, u32[]{:S(2)}) %all-to-all-start.1) | async-done | bytes 8388640 | tf_op jit(solution)/shard_map/all_to_all | solution.py:101
  524.7 0.0 copy-start.6
  524.7 8.4 copy.67
  533.1 0.0 copy-done
  533.1 0.0 copy-done.6
  533.1 10.6 %convolution_convert_fusion.1 = bf16[64,256,2,128]{3,1,2,0:T(8,128)(2,1)} fusion(bf16[64,256,2,128]{1,3,2,0:T(8,128)(2,1)} %bitcast.79, f32[64,256,128]{2,1,0:T(8,128)} %add_divide_fusion, bf16[128,128]{1,0:T(8,128)(2,1)S(1)} %copy-done, bf16[128,128]{1,0:T(8,128)(2,1)S(1)} %copy-done.6), kind=kOutput, calls=%fused_computation.20 | convolution fusion | flops 2160066560 | bytes 25231360 | tf_op jit(solution)/shard_map/sjck,lk->sjcl/dot_general | solution.py:56
  543.7 21.1 %copy.69 = bf16[64,256,2,128]{1,2,0,3:T(2,128)(2,1)} copy(bf16[64,256,2,128]{3,1,2,0:T(8,128)(2,1)} %convolution_convert_fusion.1) | data formatting | bytes 16777216 | tf_op jit(solution)/shard_map/convert_element_type | solution.py:56
  564.7 102.5 %all_to_all.69 = bf16[64,256,2,128]{1,2,0,3:T(2,128)(2,1)} all-to-all(bf16[64,256,2,128]{1,2,0,3:T(2,128)(2,1)} %copy.69), channel_id=1, replica_groups=mesh['member'=2,'wave'=4,'level'=2,'fld'=2] {'level'}, dimensions={3} | all-to-all | bytes 16777216 | tf_op jit(solution)/shard_map/all_to_all | solution.py:103
  667.2 15.9 %copy.70 = bf16[64,256,2,128]{1,3,2,0:T(8,128)(2,1)} copy(bf16[64,256,2,128]{1,2,0,3:T(2,128)(2,1)} %all_to_all.69) | data formatting | bytes 16777216 | tf_op jit(solution)/shard_map/all_to_all | solution.py:103
  683.2 8.3 copy.71
  691.5 13.3 %convert_bitcast_fusion = bf16[64,1,256,2,128]{2,0,3,4,1:T(8,128)(2,1)} fusion(bf16[128,256,2,64]{1,3,2,0:T(8,128)(2,1)} %bitcast.78, bf16[128,1,256,256]{3,2,1,0:T(8,128)(2,1)} %all-gather.2.cloned.1.call-done), kind=kOutput, calls=%fused_computation.18 | convolution fusion | flops 2151677952 | bytes 33554432 | tf_op jit(solution)/shard_map/sjcl,shrj->lhrcs/dot_general | solution.py:48
  704.7 13.5 %copy.72 = bf16[64,1,256,2,128]{4,0,3,1,2:T(8,128)(2,1)} copy(bf16[64,1,256,2,128]{2,0,3,4,1:T(8,128)(2,1)} %convert_bitcast_fusion) | data formatting | bytes 16777216 | tf_op jit(solution)/shard_map/convert_element_type | solution.py:50
  718.3 188.9 %all_to_all.70 = bf16[64,1,256,2,128]{4,0,3,1,2:T(8,128)(2,1)} all-to-all(bf16[64,1,256,2,128]{4,0,3,1,2:T(8,128)(2,1)} %copy.72), channel_id=1, replica_groups=mesh['member'=2,'wave'=4,'level'=2,'fld'=2] {'wave'}, dimensions={2} | all-to-all | bytes 16777216 | tf_op jit(solution)/shard_map/all_to_all | solution.py:105
  907.1 12.2 %copy.73 = bf16[64,1,256,2,128]{4,2,3,0,1:T(8,128)(2,1)} copy(bf16[64,1,256,2,128]{4,0,3,1,2:T(8,128)(2,1)} %all_to_all.70) | data formatting | bytes 16777216 | tf_op jit(solution)/shard_map/all_to_all | solution.py:105
  919.3 8.4 copy.87
  927.7 0.0 collective-permute-start.1
  927.7 13.4 %collective-permute-done.1 = bf16[64,1,64,2,512]{4,2,3,0,1:T(8,128)(2,1)S(1)} collective-permute-done((bf16[64,1,64,2,512]{4,2,3,0,1:T(8,128)(2,1)}, bf16[64,1,64,2,512]{4,2,3,0,1:T(8,128)(2,1)S(1)}, u32[]{:S(2)}, u32[]{:S(2)}) %collective-permute-start.1) | collective-permute-done | bytes 8388640 | tf_op jit(solution)/shard_map/ppermute | solution.py:13
  941.1 5.7 multiply_convert_fusion
  946.8 7.7 copy.75
  954.6 0.0 copy-start.3
  954.6 0.0 copy-start.5
  954.6 14.5 %reshape.141 = bf16[64,64,1024]{2,1,0:T(8,128)(2,1)} reshape(bf16[64,1,64,2,512]{4,3,2,0,1:T(2,128)(2,1)} %copy.75) | data formatting | bytes 16777216 | tf_op jit(solution)/shard_map/reshape.9
  969.1 0.0 copy-done.3
  969.1 0.0 copy-done.5
  969.1 0.0 copy-start.1
  969.1 19.4 %fusion.10 = bf16[64,1,64,1536]{3,2,1,0:T(8,128)(2,1)} fusion(bf16[64,64,1024]{2,1,0:T(8,128)(2,1)} %reshape.141, bf16[1536,512]{1,0:T(8,128)(2,1)S(1)} %copy-done.5, bf16[1536,512]{1,0:T(8,128)(2,1)S(1)} %copy-done.3), kind=kOutput, calls=%fused_computation.16 | convolution fusion | flops 12897484800 | bytes 24117248 | tf_op jit(solution)/shard_map/lhrk,gk->lhrg/dot_general | solution.py:111
  988.5 0.0 copy-done.1
  (1 shorter events, 0.0 us)
Async XLA Ops:
  6.5 526.6 %copy-start = (bf16[128,128]{1,0:T(8,128)(2,1)S(1)}, bf16[128,128]{1,0:T(8,128)(2,1)}, u32[]{:S(2)}) copy-start(bf16[128,128]{1,0:T(8,128)(2,1)} %param.13) | copy-start | bytes 98308
  6.5 403.6 %all-gather.2.cloned.1.call-start = ((), (), s32[]{:S(2)}) async-start(), calls=%async_computation.4 | async-start | bytes 25165824 | tf_op jit(solution)/shard_map/all_gather | solution.py:84
  20.6 19.8 %copy-start.2 = (bf16[1536,512]{1,0:T(8,128)(2,1)}, bf16[1536,512]{1,0:T(8,128)(2,1)S(1)}, u32[]{:S(2)}) copy-start(bf16[1536,512]{1,0:T(8,128)(2,1)S(1)} %get-tuple-element.5) | copy-start | bytes 4718596
  20.7 19.8 %copy-start.4 = (bf16[1536,512]{1,0:T(8,128)(2,1)}, bf16[1536,512]{1,0:T(8,128)(2,1)S(1)}, u32[]{:S(2)}) copy-start(bf16[1536,512]{1,0:T(8,128)(2,1)S(1)} %get-tuple-element.6) | copy-start | bytes 4718596
  64.0 13.6 %collective-permute-start = (bf16[64,1,64,2,512]{4,2,3,0,1:T(8,128)(2,1)}, bf16[64,1,64,2,512]{4,2,3,0,1:T(8,128)(2,1)}, u32[]{:S(2)}, u32[]{:S(2)}) collective-permute-start(bf16[64,1,64,2,512]{4,2,3,0,1:T(8,128)(2,1)} %copy.61), channel_id=1, source_target_pairs={{0,1},{1,0},{2,3},{3,2},{4,5},{5,4},{6,7},{7,6},{8,9},{9,8},{10,11... | collective-permute-start | bytes 25165832 | tf_op jit(solution)/shard_map/ppermute | solution.py:13
  140.9 6.2 copy-start.7
  140.9 190.6 %all-to-all-start = ((bf16[4,2,524288]{2,1,0:T(2,128)(2,1)}), bf16[4,2,524288]{2,1,0:T(2,128)(2,1)}, u32[]{:S(2)}, u32[]{:S(2)}) async-start(bf16[4,2,524288]{2,1,0:T(2,128)(2,1)} %reshape.146), calls=%async_computation | async-start | bytes 16777216 | tf_op jit(solution)/shard_map/all_to_all | solution.py:99
  425.2 7.3 copy-start.8
  425.2 99.4 %all-to-all-start.1 = ((bf16[128,256,2,64]{1,3,2,0:T(8,128)(2,1)}), bf16[128,256,2,64]{1,3,2,0:T(8,128)(2,1)}, u32[]{:S(2)}, u32[]{:S(2)}) async-start(bf16[128,256,2,64]{1,3,2,0:T(8,128)(2,1)} %fusion.18), calls=%async_computation.1 | async-start | bytes 16777216 | tf_op jit(solution)/shard_map/all_to_all | solution.py:101
  524.7 8.5 copy-start.6
  927.7 13.4 %collective-permute-start.1 = (bf16[64,1,64,2,512]{4,2,3,0,1:T(8,128)(2,1)}, bf16[64,1,64,2,512]{4,2,3,0,1:T(8,128)(2,1)S(1)}, u32[]{:S(2)}, u32[]{:S(2)}) collective-permute-start(bf16[64,1,64,2,512]{4,2,3,0,1:T(8,128)(2,1)} %bitcast.83), channel_id=1, source_target_pairs={{0,1},{1,0},{2,3},{3,2},{4,5},{5,4},{6,7},{7,6},{8,9},{9,8},{10,11... | collective-permute-start | bytes 25165832 | tf_op jit(solution)/shard_map/ppermute | solution.py:13
  954.6 14.5 %copy-start.3 = (bf16[1536,512]{1,0:T(8,128)(2,1)S(1)}, bf16[1536,512]{1,0:T(8,128)(2,1)}, u32[]{:S(2)}) copy-start(bf16[1536,512]{1,0:T(8,128)(2,1)} %copy-done.2) | copy-start | bytes 4718596
  954.6 14.5 %copy-start.5 = (bf16[1536,512]{1,0:T(8,128)(2,1)S(1)}, bf16[1536,512]{1,0:T(8,128)(2,1)}, u32[]{:S(2)}) copy-start(bf16[1536,512]{1,0:T(8,128)(2,1)} %copy-done.4) | copy-start | bytes 4718596
  969.1 19.4 %copy-start.1 = (bf16[128,128]{1,0:T(8,128)(2,1)S(1)}, bf16[128,128]{1,0:T(8,128)(2,1)}, u32[]{:S(2)}) copy-start(bf16[128,128]{1,0:T(8,128)(2,1)} %param.13) | copy-start | bytes 98308
Sparse Core Ops, SparseCore 0:
  64.6 201.2 all-gather.1
where the time goes:
time: 1010 us; the launch traced here: 996 us
  blocking collectives  291 us (29%)
  waiting for transfers between devices  288 us (29%)
  local copies, waits for them, and re-layouts  264 us (26%)
  matrix products  77.3 us (8%)
  other arithmetic  48.1 us (5%)
  between operations  13.9 us (1%)
  starting transfers between devices  13.8 us (1%)
    all_to_all x1, blocking collectives, shards(): lax.all_to_all(grid_coeffs, 'wave', split_axis=2, concat_axis=4, tiled=True)  189 us
    all_to_all x1, waiting for transfers between devices, shards(): lax.all_to_all(mirrored, 'wave', split_axis=4, concat_axis=2, tiled=True)  184 us
    all_to_all x1, blocking collectives, shards(): lax.all_to_all(solved, 'level', split_axis=3, concat_axis=0, tiled=True)  102 us
    all_to_all x1, waiting for transfers between devices, shards(): lax.all_to_all(spectral, 'level', split_axis=0, concat_axis=3, tiled=True)  77 us
    all_to_all x2, local copies, waits for them, and re-layouts, shards(): lax.all_to_all(mirrored, 'wave', split_axis=4, concat_axis=2, tiled=True)  50.5 us
    convert_element_type x1, local copies, waits for them, and re-layouts, shards(): mirrored = (mirror_part.astype(jnp.float32) + hemi_sign * fourier_rows.as...  34.4 us
    unnamed x20, local copies, waits for them, and re-layouts  32.8 us
    another operation x2, local copies, waits for them, and re-layouts  26.6 us
  transfers between devices with their start and end apart: 5, of which 4 were waited for; matrix products, arithmetic and copies ran while one was open for 16% of the time, Pallas kernels for 0%

commit v1 on v0

--- a/solution.py
+++ b/solution.py
@@ -5,6 +5,18 @@
 from jax.sharding import PartitionSpec as P
 
 tau_scale = 2.0
+
+
+def split_up(x, dim, peers):
+    dims = x.shape
+    blocks = x.reshape(*dims[:dim], peers, dims[dim] // peers, *dims[dim + 1 :])
+    return jnp.moveaxis(blocks, dim, 0)
+
+
+def joined_along(blocks, dim):
+    shape = list(blocks.shape[1:])
+    shape[dim] *= blocks.shape[0]
+    return jnp.moveaxis(blocks, 0, dim).reshape(shape)
 
 
 def partner(value, axis, stride):
@@ -96,7 +108,14 @@
     mirrored = (
         mirror_part.astype(jnp.float32) + hemi_sign * fourier_rows.astype(jnp.float32)
     ).astype(jnp.bfloat16)
-    gathered = lax.all_to_all(mirrored, "wave", split_axis=4, concat_axis=2, tiled=True)
+    size, index = (lax.axis_size("wave"), lax.axis_index("wave"))
+    blocks = split_up(mirrored, 4, size)
+    outs = [blocks[index]]
+    for step in range(1, size):
+        sent = blocks[index ^ step]
+        outs.append(lax.ppermute(sent, "wave", [(i, i ^ step) for i in range(size)]))
+    blocks = jnp.stack(outs)[index ^ jnp.arange(size)]
+    gathered = joined_along(blocks, 2)
     spectral = forward_legendre(gathered, wide_table, wide_mask)
     columns = lax.all_to_all(spectral, "level", split_axis=0, concat_axis=3, tiled=True)
     solved = implicit_solve(columns, factor, modes_in, modes_out)

time: 1010 us -> 978 us (0.968)
  waiting for transfers between devices: 288 us -> 234 us
  blocking collectives: 291 us -> 332 us
  local copies, waits for them, and re-layouts: 264 us -> 240 us
    all_to_all x1 -> x0, waiting for transfers between devices: 184 us -> none  [shards(): lax.all_to_all(mirrored, 'wave', split_axis=4, concat_axis=2, tiled=True)]
    ppermute x0 -> x3, waiting for transfers between devices: none -> 122 us  [shards(): lax.ppermute(sent, 'wave', [(i, i ^ step) for i in range(size)])]
    another operation x2 -> x7, local copies, waits for them, and re-layouts: 26.6 us -> 81 us
    all_to_all x2 -> x0, local copies, waits for them, and re-layouts: 50.5 us -> none  [shards(): lax.all_to_all(mirrored, 'wave', split_axis=4, concat_axis=2, tiled=True)]
    all_to_all x1, blocking collectives: 189 us -> 231 us  [shards(): lax.all_to_all(grid_coeffs, 'wave', split_axis=2, concat_axis=4, tiled=True)]
    convert_element_type x1 -> x0, local copies, waits for them, and re-layouts: 34.4 us -> none  [shards(): mirrored = (mirror_part.astype(jnp.float32) + hemi_sign * fourier_rows.as...]
    unnamed x20 -> x18, local copies, waits for them, and re-layouts: 32.8 us -> 0.04 us
    gather x0 -> x12, local copies, waits for them, and re-layouts: none -> 26.4 us
  transfers between devices with their start and end apart: 5 -> 7, of which waited for: 4 -> 5; matrix products, arithmetic and copies ran while one was open for 16% -> 15% of each run, Pallas kernels for 0% -> 0%
where the time goes in v1:
time: 978 us; the launch traced here: 965 us
  blocking collectives  332 us (34%)
  local copies, waits for them, and re-layouts  240 us (25%)
  waiting for transfers between devices  234 us (24%)
  matrix products  77.1 us (8%)
  other arithmetic  55.3 us (6%)
  between operations  14 us (1%)
  starting transfers between devices  13 us (1%)
    all_to_all x1, blocking collectives, shards(): lax.all_to_all(grid_coeffs, 'wave', split_axis=2, concat_axis=4, tiled=True)  231 us
    ppermute x3, waiting for transfers between devices, shards(): lax.ppermute(sent, 'wave', [(i, i ^ step) for i in range(size)])  122 us
    all_to_all x1, blocking collectives, shards(): lax.all_to_all(solved, 'level', split_axis=3, concat_axis=0, tiled=True)  101 us
    all_to_all x1, waiting for transfers between devices, shards(): lax.all_to_all(spectral, 'level', split_axis=0, concat_axis=3, tiled=True)  85.8 us
    another operation x7, local copies, waits for them, and re-layouts  81 us
    ppermute x2, waiting for transfers between devices, partner(): return lax.ppermute(value, axis, pairs)  26.4 us
    gather x12, local copies, waits for them, and re-layouts  26.4 us
    all_to_all x2, local copies, waits for them, and re-layouts, shards(): lax.all_to_all(solved, 'level', split_axis=3, concat_axis=0, tiled=True)  24.2 us
  transfers between devices with their start and end apart: 7, of which 5 were waited for; matrix products, arithmetic and copies ran while one was open for 15% of the time, Pallas kernels for 0%

profile of v1, /device:TPU:0, one launch (start us, length us, event | category | flops | bytes accessed | tf_op | source)
XLA Modules:
  0.0 965.4 jit_solution(4368614038270985137)
XLA Ops:
  6.5 0.0 all-gather.2.cloned.1.call-start
  6.5 14.1 %multiply_convert_fusion.4 = (bf16[1536,512]{1,0:T(8,128)(2,1)S(1)}, bf16[1536,512]{1,0:T(8,128)(2,1)S(1)}) fusion(s32[512]{0:T(512)} %param.9), kind=kLoop, calls=%fused_computation.32 | loop fusion | flops 11010048 | bytes 3147776 | tf_op jit(solution)/shard_map/convert
  20.6 0.0 copy-start.2
  20.7 0.8 sine_multiply_fusion
  21.5 18.9 %fusion.13 = bf16[64,64,1024]{2,1,0:T(8,128)(2,1)} fusion(bf16[64,1,64,1536]{3,2,1,0:T(8,128)(2,1)} %param.7, f32[64]{0:T(128)S(1)} %sine_multiply_fusion, bf16[1536,512]{1,0:T(8,128)(2,1)S(1)} %get-tuple-element.26, bf16[1536,512]{1,0:T(8,128)(2,1)S(1)} %get-tuple-element.25), kind=kOutput, calls=%fused_computation.25 | convolution fusion | flops 12920553472 | bytes 24117504 | tf_op jit(solution)/shard_map/lhrg,gk->lhrk/dot_general | solution.py:101
  40.4 14.5 %reshape.165 = bf16[64,1,64,2,512]{4,3,2,0,1:T(2,128)(2,1)} reshape(bf16[64,64,1024]{2,1,0:T(8,128)(2,1)} %fusion.13) | data formatting | bytes 16777216 | tf_op jit(solution)/shard_map/reshape | solution.py:104
  54.9 9.0 copy.79
  64.0 0.5 collective-permute-start
  64.5 0.0 all-gather.2.cloned.1.call-update
  64.5 13.1 %collective-permute-done = bf16[64,1,64,2,512]{4,2,3,0,1:T(8,128)(2,1)} collective-permute-done((bf16[64,1,64,2,512]{4,2,3,0,1:T(8,128)(2,1)}, bf16[64,1,64,2,512]{4,2,3,0,1:T(8,128)(2,1)}, u32[]{:S(2)}, u32[]{:S(2)}) %collective-permute-start) | collective-permute-done | bytes 8388640 | tf_op jit(solution)/shard_map/ppermute | solution.py:25
  77.6 12.1 %add_convert_fusion = bf16[64,1,64,2,512]{4,2,3,0,1:T(8,128)(2,1)} fusion(bf16[64,1,64,2,512]{4,2,3,0,1:T(8,128)(2,1)} %collective-permute-done, f32[]{:T(128)S(6)} %sub.3, bf16[64,1,64,2,512]{4,3,2,0,1:T(2,128)(2,1)} %reshape.165), kind=kLoop, calls=%fused_computation.14 | loop fusion | flops 20971520 | bytes 25165828 | tf_op jit(solution)/shard_map/convert_element_type | solution.py:110
  89.7 12.9 %reshape.166 = bf16[64,1,64,2,4,128]{5,4,2,3,0,1:T(4,128)(2,1)} reshape(bf16[64,1,64,2,512]{4,2,3,0,1:T(8,128)(2,1)} %add_convert_fusion) | data formatting | bytes 16777216 | tf_op jit(solution)/shard_map/reshape | solution.py:12
  102.6 28.6 %constant_dynamic-slice_fusion.5 = (bf16[64,1,64,2,1,128]{5,4,2,3,0,1:T(2,128)(2,1)}, bf16[64,1,64,2,1,128]{5,4,2,3,0,1:T(2,128)(2,1)S(1)}, bf16[64,1,64,2,1,128...) fusion(bf16[64,1,64,2,4,128]{5,4,2,3,0,1:T(4,128)(2,1)} %reshape.166, s32[]{:T(128)S(6)} %select_n.40, ...), kind=kLoop, calls=%fused_computation.51 | loop fusion | bytes 16777232 | tf_op jit(solution)/shard_map/dynamic-slice
  131.2 0.0 copy-start.7
  131.2 3.9 copy.116
  135.1 2.8 collective-permute-start.1
  137.9 6.9 copy.115
  144.8 2.6 collective-permute-start.2
  147.3 7.3 copy.114
  154.6 0.0 collective-permute-start.3
  154.6 0.1 dynamic_slice.17
  154.7 0.1 fusion.26
  154.8 7.8 copy.117
  162.6 59.1 %collective-permute-done.1 = bf16[64,1,64,2,128]{4,3,2,0,1:T(2,128)(2,1)} collective-permute-done((bf16[64,1,64,2,128]{4,3,2,0,1:T(2,128)(2,1)S(1)}, bf16[64,1,64,2,128]{4,3,2,0,1:T(2,128)(2,1)}, u32[]{:S(2)}, u32[]{:S(2)}) %collective-permute-start.1) | collective-permute-done | bytes 2097184 | tf_op jit(solution)/shard_map/ppermute | solution.py:116
  221.7 62.7 %collective-permute-done.2 = bf16[64,1,64,2,128]{4,3,2,0,1:T(2,128)(2,1)} collective-permute-done((bf16[64,1,64,2,128]{4,3,2,0,1:T(2,128)(2,1)}, bf16[64,1,64,2,128]{4,3,2,0,1:T(2,128)(2,1)}, u32[]{:S(2)}, u32[]{:S(2)}) %collective-permute-start.2) | collective-permute-done | bytes 2097184 | tf_op jit(solution)/shard_map/ppermute | solution.py:116
  284.4 0.0 collective-permute-done.3
  284.4 17.6 %pad_maximum_fusion = bf16[4,64,1,64,2,128]{5,4,3,2,1,0:T(2,128)(2,1)} fusion(bf16[1,64,1,64,2,128]{5,4,3,2,1,0:T(2,128)(2,1)} %bitcast.8, bf16[1,64,1,64,2,128]{5,4,3,2,1,0:T(2,128)(2,1)} %bitcast.6, bf16[1,64,1,64,2,128]{5,4,3,2,1,0:T(2,128)(2,1)} %bitcast.4, bf16[1,64,1,64,2,128]{5,4,3,2,1,0:T(2,128)(2,1)S(1)} %bitcast.101), kind=kLoop, calls=%fused_computation.21 | loop fusion | flops 12582912 | bytes 16777216 | tf_op jit(solution)/shard_map/stack | solution.py:117
  301.9 26.4 %while.1 = (s32[]{:T(128)}, bf16[4,64,1,64,2,128]{5,4,3,2,1,0:T(2,128)(2,1)}, s32[4,1]{0,1:T(1,128)S(1)}, bf16[4,64,1,64,2,128]{5,3,0,4,1,2:T(8,128)(2,1)}, s32[]{:T(128)}) while((s32[]{:T(128)}, bf16[4,64,1,64,2,128]{5,4,3,2,1,0:T(2,128)(2,1)}, s32[4,1]{0,1:T(1,128)S(1)}, bf16[4,64,1,64,2,128]{5,3,0,4,1,2:T(8,128)(2,1)}, s32[]{:T(128)}) %tuple.20), condition=%wide.while_cond, body=%wide.while_body.sunk | while | flops 2 | bytes 8389197 | solution.py:117
  301.9 0.6 constant_dynamic-slice_fusion.8
  302.5 4.0 constant_dynamic-slice_fusion.9
  306.6 1.9 copy_dynamic-update-slice_fusion.2
  308.5 0.6 constant_dynamic-slice_fusion.8
  309.1 4.0 constant_dynamic-slice_fusion.9
  313.1 2.0 copy_dynamic-update-slice_fusion.2
  315.1 0.6 constant_dynamic-slice_fusion.8
  315.7 4.0 constant_dynamic-slice_fusion.9
  319.7 2.0 copy_dynamic-update-slice_fusion.2
  321.7 0.6 constant_dynamic-slice_fusion.8
  322.3 4.0 constant_dynamic-slice_fusion.9
  326.4 2.0 copy_dynamic-update-slice_fusion.2
  328.4 12.1 %copy.86 = bf16[64,256,2,128]{1,0,2,3:T(8,128)(2,1)} copy(bf16[64,256,2,128]{3,1,2,0:T(8,128)(2,1)} %bitcast.99) | data formatting | bytes 16777216 | tf_op jit(solution)/shard_map/reshape.8
  340.5 15.1 %fusion.18 = bf16[128,256,2,64]{1,3,2,0:T(8,128)(2,1)} fusion(f32[128,256]{1,0:T(8,128)S(1)} %fusion.26, bf16[64,256,2,128]{1,0,2,3:T(8,128)(2,1)} %copy.86, bf16[128,1,256,256]{3,2,1,0:T(8,128)(2,1)} %all-gather.2.cloned.1.call-done), kind=kOutput, calls=%fused_computation.26 | convolution fusion | flops 2155872256 | bytes 33685504 | tf_op jit(solution)/shard_map/lhrcs,shrj->sjcl/dot_general | solution.py:53
  355.6 7.1 all-to-all-start
  362.7 0.1 dynamic_slice.18
  362.8 0.1 multiply_multiply_fusion
  362.9 4.7 add_divide_fusion
  367.6 85.8 %all-to-all-done = bf16[128,256,2,64]{1,3,2,0:T(8,128)(2,1)} async-done(((bf16[128,256,2,64]{1,3,2,0:T(8,128)(2,1)}), bf16[128,256,2,64]{1,3,2,0:T(8,128)(2,1)}, u32[]{:S(2)}, u32[]{:S(2)}) %all-to-all-start) | async-done | bytes 8388640 | tf_op jit(solution)/shard_map/all_to_all | solution.py:120
  453.5 8.4 copy.87
  461.9 10.4 %convolution_convert_fusion.1 = bf16[64,256,2,128]{3,1,2,0:T(8,128)(2,1)} fusion(bf16[64,256,2,128]{1,3,2,0:T(8,128)(2,1)} %bitcast.97, f32[64,256,128]{2,1,0:T(8,128)} %add_divide_fusion, bf16[128,128]{1,0:T(8,128)(2,1)S(1)} %copy-done, bf16[128,128]{1,0:T(8,128)(2,1)S(1)} %copy-done.6), kind=kOutput, calls=%fused_computation.24 | convolution fusion | flops 2160066560 | bytes 25231360 | tf_op jit(solution)/shard_map/sjck,lk->sjcl/dot_general | solution.py:68
  472.3 21.1 %copy.89 = bf16[64,256,2,128]{1,2,0,3:T(2,128)(2,1)} copy(bf16[64,256,2,128]{3,1,2,0:T(8,128)(2,1)} %convolution_convert_fusion.1) | data formatting | bytes 16777216 | tf_op jit(solution)/shard_map/convert_element_type | solution.py:68
  493.3 100.9 %all_to_all.54 = bf16[64,256,2,128]{1,2,0,3:T(2,128)(2,1)} all-to-all(bf16[64,256,2,128]{1,2,0,3:T(2,128)(2,1)} %copy.89), channel_id=1, replica_groups=mesh['member'=2,'wave'=4,'level'=2,'fld'=2] {'level'}, dimensions={3} | all-to-all | bytes 16777216 | tf_op jit(solution)/shard_map/all_to_all | solution.py:122
  594.3 15.9 %copy.90 = bf16[64,256,2,128]{1,3,2,0:T(8,128)(2,1)} copy(bf16[64,256,2,128]{1,2,0,3:T(2,128)(2,1)} %all_to_all.54) | data formatting | bytes 16777216 | tf_op jit(solution)/shard_map/all_to_all | solution.py:122
  610.2 8.3 copy.91
  618.5 13.3 %convert_bitcast_fusion = bf16[64,1,256,2,128]{2,0,3,4,1:T(8,128)(2,1)} fusion(bf16[128,256,2,64]{1,3,2,0:T(8,128)(2,1)} %bitcast.96, bf16[128,1,256,256]{3,2,1,0:T(8,128)(2,1)} %all-gather.2.cloned.1.call-done), kind=kOutput, calls=%fused_computation.22 | convolution fusion | flops 2151677952 | bytes 33554432 | tf_op jit(solution)/shard_map/sjcl,shrj->lhrcs/dot_general | solution.py:60
  631.8 13.5 %copy.92 = bf16[64,1,256,2,128]{4,0,3,1,2:T(8,128)(2,1)} copy(bf16[64,1,256,2,128]{2,0,3,4,1:T(8,128)(2,1)} %convert_bitcast_fusion) | data formatting | bytes 16777216 | tf_op jit(solution)/shard_map/convert_element_type | solution.py:62
  645.3 231.4 %all_to_all.55 = bf16[64,1,256,2,128]{4,0,3,1,2:T(8,128)(2,1)} all-to-all(bf16[64,1,256,2,128]{4,0,3,1,2:T(8,128)(2,1)} %copy.92), channel_id=1, replica_groups=mesh['member'=2,'wave'=4,'level'=2,'fld'=2] {'wave'}, dimensions={2} | all-to-all | bytes 16777216 | tf_op jit(solution)/shard_map/all_to_all | solution.py:124
  876.7 12.2 %copy.93 = bf16[64,1,256,2,128]{4,2,3,0,1:T(8,128)(2,1)} copy(bf16[64,1,256,2,128]{4,0,3,1,2:T(8,128)(2,1)} %all_to_all.55) | data formatting | bytes 16777216 | tf_op jit(solution)/shard_map/all_to_all | solution.py:124
  888.9 8.4 copy.113
  897.3 0.0 collective-permute-start.4
  897.3 13.4 %collective-permute-done.4 = bf16[64,1,64,2,512]{4,2,3,0,1:T(8,128)(2,1)S(1)} collective-permute-done((bf16[64,1,64,2,512]{4,2,3,0,1:T(8,128)(2,1)}, bf16[64,1,64,2,512]{4,2,3,0,1:T(8,128)(2,1)S(1)}, u32[]{:S(2)}, u32[]{:S(2)}) %collective-permute-start.4) | collective-permute-done | bytes 8388640 | tf_op jit(solution)/shard_map/ppermute | solution.py:25
  910.7 5.7 multiply_convert_fusion
  916.5 7.7 copy.95
  924.2 14.5 %reshape.169 = bf16[64,64,1024]{2,1,0:T(8,128)(2,1)} reshape(bf16[64,1,64,2,512]{4,3,2,0,1:T(2,128)(2,1)} %copy.95) | data formatting | bytes 16777216 | tf_op jit(solution)/shard_map/reshape.11
  938.7 19.4 %fusion.10 = bf16[64,1,64,1536]{3,2,1,0:T(8,128)(2,1)} fusion(bf16[64,64,1024]{2,1,0:T(8,128)(2,1)} %reshape.169, bf16[1536,512]{1,0:T(8,128)(2,1)S(1)} %copy-done.5, bf16[1536,512]{1,0:T(8,128)(2,1)S(1)} %copy-done.3), kind=kOutput, calls=%fused_computation.19 | convolution fusion | flops 12897484800 | bytes 24117248 | tf_op jit(solution)/shard_map/lhrk,gk->lhrg/dot_general | solution.py:130
  (20 shorter events, 0.0 us)
Async XLA Ops:
  6.5 455.4 %copy-start = (bf16[128,128]{1,0:T(8,128)(2,1)S(1)}, bf16[128,128]{1,0:T(8,128)(2,1)}, u32[]{:S(2)}) copy-start(bf16[128,128]{1,0:T(8,128)(2,1)} %param.13) | copy-start | bytes 98308
  6.5 334.0 %all-gather.2.cloned.1.call-start = ((), (), s32[]{:S(2)}) async-start(), calls=%async_computation.3 | async-start | bytes 25165824 | tf_op jit(solution)/shard_map/all_gather | solution.py:96
  20.6 19.8 %copy-start.2 = (bf16[1536,512]{1,0:T(8,128)(2,1)}, bf16[1536,512]{1,0:T(8,128)(2,1)S(1)}, u32[]{:S(2)}) copy-start(bf16[1536,512]{1,0:T(8,128)(2,1)S(1)} %get-tuple-element.25) | copy-start | bytes 4718596
  20.7 19.8 %copy-start.4 = (bf16[1536,512]{1,0:T(8,128)(2,1)}, bf16[1536,512]{1,0:T(8,128)(2,1)S(1)}, u32[]{:S(2)}) copy-start(bf16[1536,512]{1,0:T(8,128)(2,1)S(1)} %get-tuple-element.26) | copy-start | bytes 4718596
  64.0 13.6 %collective-permute-start = (bf16[64,1,64,2,512]{4,2,3,0,1:T(8,128)(2,1)}, bf16[64,1,64,2,512]{4,2,3,0,1:T(8,128)(2,1)}, u32[]{:S(2)}, u32[]{:S(2)}) collective-permute-start(bf16[64,1,64,2,512]{4,2,3,0,1:T(8,128)(2,1)} %copy.79), channel_id=1, source_target_pairs={{0,1},{1,0},{2,3},{3,2},{4,5},{5,4},{6,7},{7,6},{8,9},{9,8},{10,11... | collective-permute-start | bytes 25165832 | tf_op jit(solution)/shard_map/ppermute | solution.py:25
  131.2 23.4 %copy-start.7 = (s32[512]{0:T(512)S(1)}, s32[512]{0:T(512)}, u32[]{:S(2)}) copy-start(s32[512]{0:T(512)} %param.9) | copy-start | bytes 6148
  135.1 86.6 %collective-permute-start.1 = (bf16[64,1,64,2,128]{4,3,2,0,1:T(2,128)(2,1)S(1)}, bf16[64,1,64,2,128]{4,3,2,0,1:T(2,128)(2,1)}, u32[]{:S(2)}, u32[]{:S(2)}) collective-permute-start(bf16[64,1,64,2,128]{4,3,2,0,1:T(2,128)(2,1)S(1)} %bitcast.102), channel_id=1, source_target_pairs={{0,4},{4,0},{8,12},{12,8},{1,5},{5,1},{9,13},{13,9},{2,6},{6,2},{1... | collective-permute-start | bytes 6291464 | tf_op jit(solution)/shard_map/ppermute | solution.py:116
  144.8 139.6 %collective-permute-start.2 = (bf16[64,1,64,2,128]{4,3,2,0,1:T(2,128)(2,1)}, bf16[64,1,64,2,128]{4,3,2,0,1:T(2,128)(2,1)}, u32[]{:S(2)}, u32[]{:S(2)}) collective-permute-start(bf16[64,1,64,2,128]{4,3,2,0,1:T(2,128)(2,1)} %bitcast.89), channel_id=1, source_target_pairs={{0,8},{4,12},{8,0},{12,4},{1,9},{5,13},{9,1},{13,5},{2,10},{6,14},... | collective-permute-start | bytes 6291464 | tf_op jit(solution)/shard_map/ppermute | solution.py:116
  154.6 129.8 %collective-permute-start.3 = (bf16[64,1,64,2,128]{4,3,2,0,1:T(2,128)(2,1)}, bf16[64,1,64,2,128]{4,3,2,0,1:T(2,128)(2,1)}, u32[]{:S(2)}, u32[]{:S(2)}) collective-permute-start(bf16[64,1,64,2,128]{4,3,2,0,1:T(2,128)(2,1)} %bitcast.88), channel_id=1, source_target_pairs={{0,12},{4,8},{8,4},{12,0},{1,13},{5,9},{9,5},{13,1},{2,14},{6,10},... | collective-permute-start | bytes 6291464 | tf_op jit(solution)/shard_map/ppermute | solution.py:116
  355.6 7.3 copy-start.8
  355.6 97.9 %all-to-all-start = ((bf16[128,256,2,64]{1,3,2,0:T(8,128)(2,1)}), bf16[128,256,2,64]{1,3,2,0:T(8,128)(2,1)}, u32[]{:S(2)}, u32[]{:S(2)}) async-start(bf16[128,256,2,64]{1,3,2,0:T(8,128)(2,1)} %fusion.18), calls=%async_computation | async-start | bytes 16777216 | tf_op jit(solution)/shard_map/all_to_all | solution.py:120
  453.5 8.5 copy-start.6
  897.3 13.4 %collective-permute-start.4 = (bf16[64,1,64,2,512]{4,2,3,0,1:T(8,128)(2,1)}, bf16[64,1,64,2,512]{4,2,3,0,1:T(8,128)(2,1)S(1)}, u32[]{:S(2)}, u32[]{:S(2)}) collective-permute-start(bf16[64,1,64,2,512]{4,2,3,0,1:T(8,128)(2,1)} %bitcast.100), channel_id=1, source_target_pairs={{0,1},{1,0},{2,3},{3,2},{4,5},{5,4},{6,7},{7,6},{8,9},{9,8},{10,11... | collective-permute-start | bytes 25165832 | tf_op jit(solution)/shard_map/ppermute | solution.py:25
  924.2 14.5 %copy-start.3 = (bf16[1536,512]{1,0:T(8,128)(2,1)S(1)}, bf16[1536,512]{1,0:T(8,128)(2,1)}, u32[]{:S(2)}) copy-start(bf16[1536,512]{1,0:T(8,128)(2,1)} %copy-done.2) | copy-start | bytes 4718596
  924.2 14.5 %copy-start.5 = (bf16[1536,512]{1,0:T(8,128)(2,1)S(1)}, bf16[1536,512]{1,0:T(8,128)(2,1)}, u32[]{:S(2)}) copy-start(bf16[1536,512]{1,0:T(8,128)(2,1)} %copy-done.4) | copy-start | bytes 4718596
  938.7 19.4 %copy-start.1 = (bf16[128,128]{1,0:T(8,128)(2,1)S(1)}, bf16[128,128]{1,0:T(8,128)(2,1)}, u32[]{:S(2)}) copy-start(bf16[128,128]{1,0:T(8,128)(2,1)} %param.13) | copy-start | bytes 98308
Sparse Core Ops, SparseCore 0:
  64.6 201.2 all-gather.1
